TPU v7x, 128 devices: a whole 4x4x4 slice. The times are simulated.
128 devices in a mesh: dp: 2 (over x_lo), seq: 16 (over z, y), mp: 4 (over x_hi, core).
Axes of the slice: x: 4 (x_hi: 2, x_lo: 2; x = x_hi * 2 + x_lo), y: 4, z: 4, core: 2. Of those that a mesh axis runs over, the one named last changes fastest.
Arguments:
- shortening_input: bfloat16 [2, 32768, 2048], P('dp', ('seq', 'mp')), may hold values from -16 to 16
- coarse_grad: bfloat16 [2, 8192, 4096], P('dp', 'seq', 'mp'), may hold values from -6 to 6
- weight_copy: bfloat16 [2, 4096, 4096], P('dp', None, 'mp'), may hold values from -0.0625 to 0.0625
- master: float32 [2, 4096, 4096], P('dp', 'seq', 'mp'), may hold values from -3 to 3
- moment: float32 [2, 4096, 4096], P('dp', 'seq', 'mp'), may hold values from -3 to 3
- second: float32 [2, 4096, 4096], P('dp', 'seq', 'mp'), may hold values from 0.05 to 5
Outputs:
- act_grad: bfloat16 [2, 32768, 2048], P('dp', ('seq', 'mp'))
- new_master: float32 [2, 4096, 4096], P('dp', 'seq', 'mp')
- new_moment: float32 [2, 4096, 4096], P('dp', 'seq', 'mp')
- new_second: float32 [2, 4096, 4096], P('dp', 'seq', 'mp')
- new_weight: bfloat16 [2, 4096, 4096], P(None, 'seq', 'mp')
All inputs are finite; a program needn't handle non-finite values.
Results may differ from a plain program's by a relative error of at most 0.009.
Values may be sent and summed in bfloat16 or wider, within the bound.
A program may use at most 128 MiB of HBM per device.

v0:
```python
import math
import jax
import jax.numpy as jnp
from jax import lax
from jax.sharding import PartitionSpec as P

SHORT = 4
first_beta = 0.9
second_beta = 0.95
first_fix = 1.0 - 0.9**10
second_fix = 1.0 - 0.95**10
adam_eps = 1e-08
learn_rate = 0.05
weight_decay = 0.1


def shifted(value, axis, steps):
    count = lax.axis_size(axis)
    initial, last = (max(0, -steps), min(count, count - steps))
    return lax.ppermute(value, axis, [(source, source + steps) for source in range(initial, last)])


def per_device(shortening_input, coarse_grad, weight_copy, master, moment, second):
    fine_rows = shortening_input[0]
    rows_dev = fine_rows.shape[0]
    features = fine_rows.shape[1]
    grad_cols = coarse_grad[0]
    coarse_rows = grad_cols.shape[0]
    wide_rows = SHORT * features
    whole_copy = lax.all_gather(weight_copy, "dp", axis=0, tiled=True)
    weights = whole_copy.reshape(wide_rows, whole_copy.shape[2])
    summed = (
        lax.psum_scatter(
            lax.dot_general(
                grad_cols, weights, (((1,), (1,)), ((), ())), preferred_element_type=jnp.float32
            ).astype(jnp.bfloat16),
            "mp",
            scatter_dimension=0,
            tiled=True,
        )
        .astype(jnp.float32)
        .reshape(rows_dev, features)
    )
    later_rows = shifted(summed[: SHORT - 1], ("seq", "mp"), -1)
    act_grad = jnp.concatenate([summed[SHORT - 1 :], later_rows], axis=0).astype(jnp.bfloat16)
    gathered = lax.all_gather(fine_rows, "mp", axis=0, tiled=True).reshape(coarse_rows, wide_rows)
    owned_rows = lax.psum_scatter(
        lax.dot_general(
            gathered, grad_cols, (((0,), (0,)), ((), ())), preferred_element_type=jnp.float32
        ).astype(jnp.bfloat16),
        ("dp", "seq"),
        scatter_dimension=0,
        tiled=True,
    ).astype(jnp.float32)
    grad_scale = 1.0 / math.sqrt(lax.axis_size("dp") * coarse_rows * lax.axis_size("seq"))
    gradient = (owned_rows * grad_scale).reshape(master.shape)
    new_moment = first_beta * moment + (1.0 - first_beta) * gradient
    new_second = second_beta * second + (1.0 - second_beta) * gradient * gradient
    step_ratio = new_moment / first_fix / (jnp.sqrt(new_second / second_fix) + adam_eps)
    new_master = master - learn_rate * (step_ratio + weight_decay * master)
    new_weight = lax.all_gather(new_master.astype(jnp.bfloat16), "dp", axis=0, tiled=True)
    return (act_grad[None], new_master, new_moment, new_second, new_weight)


def solution(mesh):
    return jax.shard_map(
        per_device,
        mesh=mesh,
        in_specs=(
            P("dp", ("seq", "mp"), None),
            P("dp", "seq", "mp"),
            P("dp", None, "mp"),
            P("dp", "seq", "mp"),
            P("dp", "seq", "mp"),
            P("dp", "seq", "mp"),
        ),
        out_specs=(
            P("dp", ("seq", "mp"), None),
            P("dp", "seq", "mp"),
            P("dp", "seq", "mp"),
            P("dp", "seq", "mp"),
            P(None, "seq", "mp"),
        ),
        check_vma=False,
    )
```

profile of v0, /device:TPU:1, one launch (start us, length us, event | category | flops | bytes accessed | tf_op | source)
XLA Modules:
  0.0 598.7 jit_solution(8087881129983664939)
XLA Ops:
  7.2 0.0 copy-start
  7.2 0.0 all-gather.9.cloned.1.call-start
  7.2 0.7 all-gather.9.cloned.1.call-update
  7.9 0.0 all-gather.5.cloned.1.call-start
  8.0 0.7 all-gather.5.cloned.1.call-update
  8.7 0.0 reduce-scatter.5.cloned.1.call-start
  8.7 66.9 %all-gather.9.cloned.1.call-done = bf16[1,2048,2048]{2,1,0:T(8,128)(2,1)} async-done(((bf16[1,512,2048]{2,1,0:T(8,128)(2,1)}), bf16[1,2048,2048]{2,1,0:T(8,128)(2,1)}) %all-gather.9.cloned.1.call-update) | async-done | bytes 8388624 | tf_op jit(solution)/shard_map/all_gather | solution.py:46
  75.6 15.1 %reshape.57 = bf16[512,8192]{1,0:T(8,128)(2,1)} reshape(bf16[1,2048,2048]{2,1,0:T(8,128)(2,1)} %all-gather.9.cloned.1.call-done) | data formatting | bytes 16777216 | tf_op jit(solution)/shard_map/reshape | solution.py:46
  90.7 0.0 copy-done
  90.7 17.8 %convolution_convert_fusion = bf16[8192,1024]{1,0:T(8,128)(2,1)} fusion(bf16[512,8192]{1,0:T(8,128)(2,1)} %reshape.57, bf16[1,512,1024]{2,1,0:T(8,128)(2,1)S(1)} %copy-done), kind=kOutput, calls=%fused_computation | convolution fusion | flops 8598323200 | bytes 26214400 | tf_op jit(solution)/shard_map/dot_general | solution.py:48
  108.4 0.0 reduce-scatter.5.cloned.1.call-update
  108.4 0.0 reduce-scatter.3.cloned.1.call-start
  108.5 169.0 %all-gather.5.cloned.1.call-done = bf16[2,4096,1024]{2,1,0:T(8,128)(2,1)} async-done(((bf16[1,4096,1024]{2,1,0:T(8,128)(2,1)}), bf16[2,4096,1024]{2,1,0:T(8,128)(2,1)}) %all-gather.5.cloned.1.call-update) | async-done | bytes 16777232 | tf_op jit(solution)/shard_map/all_gather | solution.py:30
  277.5 29.6 %convolution_convert_fusion.1 = bf16[512,8192]{1,0:T(8,128)(2,1)} fusion(bf16[8192,1024]{1,0:T(8,128)(2,1)} %bitcast.24, bf16[1,512,1024]{2,1,0:T(8,128)(2,1)S(1)} %copy-done), kind=kOutput, calls=%fused_computation.1 | convolution fusion | flops 8594128896 | bytes 26214400 | tf_op jit(solution)/shard_map/dot_general | solution.py:34
  307.1 0.0 copy-start.2
  307.1 0.0 copy-start.3
  307.1 0.0 reduce-scatter.3.cloned.1.call-update
  307.1 0.0 all-gather.7.cloned.1.call-start
  307.2 160.9 %reduce-scatter.5.cloned.1.call-done = bf16[256,1024]{1,0:T(8,128)(2,1)} async-done(((bf16[8192,1024]{1,0:T(8,128)(2,1)}), bf16[256,1024]{1,0:T(8,128)(2,1)}) %reduce-scatter.5.cloned.1.call-update) | async-done | bytes 524304 | tf_op jit(solution)/shard_map/reduce_scatter | solution.py:47
  468.1 0.0 copy-done.2
  468.1 0.0 copy-done.3
  468.1 3.9 fusion.7
  472.0 0.0 all-gather.7.cloned.1.call-update
  472.0 92.6 %reduce-scatter.3.cloned.1.call-done = bf16[128,8192]{1,0:T(8,128)(2,1)} async-done(((bf16[512,8192]{1,0:T(8,128)(2,1)}), bf16[128,8192]{1,0:T(8,128)(2,1)}) %reduce-scatter.3.cloned.1.call-update) | async-done | bytes 2097168 | tf_op jit(solution)/shard_map/reduce_scatter | solution.py:33
  564.5 3.4 reshape.56
  567.9 2.7 collective-permute-start
  570.7 0.5 slice_bitcast_fusion
  571.2 3.3 collective-permute-done
  574.5 1.5 pad_maximum_fusion
  576.0 13.9 %all-gather.7.cloned.1.call-done = bf16[2,256,1024]{2,1,0:T(8,128)(2,1)} async-done(((bf16[1,256,1024]{2,1,0:T(8,128)(2,1)}), bf16[2,256,1024]{2,1,0:T(8,128)(2,1)}) %all-gather.7.cloned.1.call-update) | async-done | bytes 1048592 | tf_op jit(solution)/shard_map/all_gather | solution.py:61
  589.9 2.3 copy.12
  592.2 0.0 copy-done.1
  (2 shorter events, 0.0 us)
Async XLA Ops:
  7.2 83.5 %copy-start = (bf16[1,512,1024]{2,1,0:T(8,128)(2,1)S(1)}, bf16[1,512,1024]{2,1,0:T(8,128)(2,1)}, u32[]{:S(2)}) copy-start(bf16[1,512,1024]{2,1,0:T(8,128)(2,1)} %param.7) | copy-start | bytes 3145732
  7.2 68.4 %all-gather.9.cloned.1.call-start = ((), (), s32[]{:S(2)}) async-start(), calls=%async_computation.6 | async-start | bytes 10485760 | tf_op jit(solution)/shard_map/all_gather | solution.py:46
  7.9 269.6 %all-gather.5.cloned.1.call-start = ((), (), s32[]{:S(2)}) async-start(), calls=%async_computation.2 | async-start | bytes 25165824 | tf_op jit(solution)/shard_map/all_gather | solution.py:30
  8.7 459.4 %reduce-scatter.5.cloned.1.call-start = ((), (), s32[]{:S(2)}) async-start(), calls=%async_computation.4 | async-start | bytes 17301504 | tf_op jit(solution)/shard_map/reduce_scatter | solution.py:47
  108.4 456.1 %reduce-scatter.3.cloned.1.call-start = ((), (), s32[]{:S(2)}) async-start(), calls=%async_computation.3 | async-start | bytes 10485760 | tf_op jit(solution)/shard_map/reduce_scatter | solution.py:33
  307.1 161.0 %copy-start.2 = (f32[1,256,1024]{2,1,0:T(8,128)S(1)}, f32[1,256,1024]{2,1,0:T(8,128)}, u32[]{:S(2)}) copy-start(f32[1,256,1024]{2,1,0:T(8,128)} %param.9) | copy-start | bytes 3145732
  307.1 161.0 %copy-start.3 = (f32[1,256,1024]{2,1,0:T(8,128)S(1)}, f32[1,256,1024]{2,1,0:T(8,128)}, u32[]{:S(2)}) copy-start(f32[1,256,1024]{2,1,0:T(8,128)} %param.10) | copy-start | bytes 3145732
  307.1 282.8 %all-gather.7.cloned.1.call-start = ((), (), s32[]{:S(2)}) async-start(), calls=%async_computation.5 | async-start | bytes 1572864 | tf_op jit(solution)/shard_map/all_gather | solution.py:61
  468.1 124.1 %copy-start.1 = (bf16[1,512,1024]{2,1,0:T(8,128)(2,1)S(1)}, bf16[1,512,1024]{2,1,0:T(8,128)(2,1)}, u32[]{:S(2)}) copy-start(bf16[1,512,1024]{2,1,0:T(8,128)(2,1)} %param.7) | copy-start | bytes 3145732
  567.9 6.6 %collective-permute-start = (bf16[3,2048]{1,0:T(4,128)(2,1)S(1)}, bf16[3,2048]{1,0:T(4,128)(2,1)S(1)}, u32[]{:S(2)}, u32[]{:S(2)}) collective-permute-start(bf16[3,2048]{1,0:T(4,128)(2,1)S(1)} %slice.18), channel_id=1, source_target_pairs={{1,0},{2,1},{3,2},{4,3},{5,4},{6,5},{7,6},{8,7},{9,8},{10,9},{11,1... | collective-permute-start | bytes 36872 | tf_op jit(solution)/shard_map/ppermute | solution.py:20
Sparse Core Ops, SparseCore 0:
  9.7 65.8 all-gather.8
  77.2 200.2 all-gather.4
  279.9 188.1 reduce-scatter.4
  470.6 93.8 reduce-scatter.2
  566.6 23.2 all-gather.6
where the time goes:
time: 599 us
  waiting for transfers between devices  508 us (85%)
  matrix products  47.4 us (8%)
  local copies, waits for them, and re-layouts  21.2 us (4%)
  between operations  13.8 us (2%)
    all_gather x1, waiting for transfers between devices, per_device(): whole_copy = lax.all_gather(weight_copy, 'dp', axis=0, tiled=True)  169 us
    reduce_scatter x1, waiting for transfers between devices, per_device(): lax.psum_scatter(lax.dot_general(gathered, grad_cols, (((0,), (0,)), ((),...  161 us
    reduce_scatter x1, waiting for transfers between devices, per_device(): lax.psum_scatter(lax.dot_general(grad_cols, weights, (((1,), (1,)), ((),...  92.6 us
    all_gather x1, waiting for transfers between devices, per_device(): lax.all_gather(fine_rows, 'mp', axis=0, tiled=True)  66.9 us
    dot_general x1, matrix products, per_device(): lax.dot_general(grad_cols, weights, (((1,), (1,)), ((), ())), preferred_e...  29.6 us
    dot_general x1, matrix products, per_device(): lax.dot_general(gathered, grad_cols, (((0,), (0,)), ((), ())), preferred_...  17.8 us
    reshape x1, local copies, waits for them, and re-layouts, per_device(): lax.all_gather(fine_rows, 'mp', axis=0, tiled=True)  15.1 us
    all_gather x1, waiting for transfers between devices, per_device(): lax.all_gather(new_master.astype(jnp.bfloat16), 'dp', axis=0, tiled=True)  13.9 us
  transfers between devices with their start and end apart: 6, of which 6 were waited for; matrix products, arithmetic and copies ran while one was open for 12% of the time, Pallas kernels for 0%

commit v1 on v0

--- a/solution.py
+++ b/solution.py
@@ -43,7 +43,9 @@
     )
     later_rows = shifted(summed[: SHORT - 1], ("seq", "mp"), -1)
     act_grad = jnp.concatenate([summed[SHORT - 1 :], later_rows], axis=0).astype(jnp.bfloat16)
-    gathered = lax.all_gather(fine_rows, "mp", axis=0, tiled=True).reshape(coarse_rows, wide_rows)
+    gathered = jnp.concatenate(
+        lax.all_to_all(jnp.stack([fine_rows] * lax.axis_size("mp")), "mp", 0, 0), axis=0
+    ).reshape(coarse_rows, wide_rows)
     owned_rows = lax.psum_scatter(
         lax.dot_general(
             gathered, grad_cols, (((0,), (0,)), ((), ())), preferred_element_type=jnp.float32

time: 599 us -> 585 us (0.977)
  waiting for transfers between devices: 508 us -> 319 us
  blocking collectives: 0 us -> 173 us
    all_to_all x0 -> x1, blocking collectives: none -> 173 us  [per_device(): lax.all_to_all(jnp.stack([fine_rows] * lax.axis_size('mp')), 'mp', 0, 0)]
    all_gather x1, waiting for transfers between devices: 169 us -> 74.1 us  [per_device(): whole_copy = lax.all_gather(weight_copy, 'dp', axis=0, tiled=True)]
    all_gather x1 -> x0, waiting for transfers between devices: 66.9 us -> none  [per_device(): lax.all_gather(fine_rows, 'mp', axis=0, tiled=True)]
    another operation x0 -> x2, local copies, waits for them, and re-layouts: none -> 15.7 us  [the longest x1 14.6 us: per_device(): gathered = jnp.concatenate(lax.all_to_all(jnp.stack([fine_rows] * lax.axi...]
    reshape x1 -> x0, local copies, waits for them, and re-layouts: 15.1 us -> none  [per_device(): lax.all_gather(fine_rows, 'mp', axis=0, tiled=True)]
    all_gather x1, waiting for transfers between devices: 13.9 us -> 0.01 us  [per_device(): lax.all_gather(new_master.astype(jnp.bfloat16), 'dp', axis=0, tiled=True)]
    reduce_scatter x1, waiting for transfers between devices: 161 us -> 148 us  [per_device(): lax.psum_scatter(lax.dot_general(gathered, grad_cols, (((0,), (0,)), ((),...]
  transfers between devices with their start and end apart: 6 -> 5, of which waited for: 6 -> 4; matrix products, arithmetic and copies ran while one was open for 12% -> 12% of each run, Pallas kernels for 0% -> 0%
where the time goes in v1:
time: 585 us; the launch traced here: 584 us
  waiting for transfers between devices  319 us (55%)
  blocking collectives  173 us (30%)
  matrix products  45.6 us (8%)
  local copies, waits for them, and re-layouts  22.8 us (4%)
  between operations  15.6 us (3%)
    all_to_all x1, blocking collectives, per_device(): lax.all_to_all(jnp.stack([fine_rows] * lax.axis_size('mp')), 'mp', 0, 0)  173 us
    reduce_scatter x1, waiting for transfers between devices, per_device(): lax.psum_scatter(lax.dot_general(gathered, grad_cols, (((0,), (0,)), ((),...  148 us
    reduce_scatter x1, waiting for transfers between devices, per_device(): lax.psum_scatter(lax.dot_general(grad_cols, weights, (((1,), (1,)), ((),...  93.4 us
    all_gather x1, waiting for transfers between devices, per_device(): whole_copy = lax.all_gather(weight_copy, 'dp', axis=0, tiled=True)  74.1 us
    dot_general x1, matrix products, per_device(): lax.dot_general(grad_cols, weights, (((1,), (1,)), ((), ())), preferred_e...  29.6 us
    dot_general x1, matrix products, per_device(): lax.dot_general(gathered, grad_cols, (((0,), (0,)), ((), ())), preferred_...  15.9 us
    another operation x1, local copies, waits for them, and re-layouts, per_device(): gathered = jnp.concatenate(lax.all_to_all(jnp.stack([fine_rows] * lax.axi...  14.6 us
  transfers between devices with their start and end apart: 5, of which 4 were waited for; matrix products, arithmetic and copies ran while one was open for 12% of the time, Pallas kernels for 0%

profile of v1, /device:TPU:1, one launch (start us, length us, event | category | flops | bytes accessed | tf_op | source)
XLA Modules:
  0.0 584.2 jit_solution(17745096046316756937)
XLA Ops:
  8.0 0.0 copy-start
  8.0 0.0 copy-start.2
  8.0 0.0 all-gather.3.cloned.1.call-start
  8.1 0.7 all-gather.3.cloned.1.call-update
  8.8 0.0 reduce-scatter.5.cloned.1.call-start
  8.8 0.9 copy-done.2
  9.7 1.1 stack.3
  10.8 172.8 %all_to_all.5 = bf16[4,512,2048]{2,1,0:T(8,128)(2,1)} all-to-all(bf16[4,512,2048]{2,1,0:T(8,128)(2,1)S(1)} %stack.3), channel_id=1, replica_groups=mesh['dp'=2,'seq'=16,'mp'=4] {'mp'}, dimensions={0} | all-to-all | bytes 16777216 | tf_op jit(solution)/shard_map/all_to_all | solution.py:47
  183.6 14.6 %reshape_reshape.3 = bf16[512,8192]{1,0:T(8,128)(2,1)} reshape(bf16[4,512,2048]{2,1,0:T(8,128)(2,1)} %all_to_all.5) | data formatting | bytes 16777216 | tf_op jit(solution)/shard_map/reshape;reshape | solution.py:48
  198.2 0.0 copy-done
  198.2 15.9 %convolution_convert_fusion = bf16[8192,1024]{1,0:T(8,128)(2,1)} fusion(bf16[512,8192]{1,0:T(8,128)(2,1)} %reshape_reshape.3, bf16[1,512,1024]{2,1,0:T(8,128)(2,1)S(1)} %copy-done), kind=kOutput, calls=%fused_computation | convolution fusion | flops 8598323200 | bytes 26214400 | tf_op jit(solution)/shard_map/dot_general | solution.py:50
  214.1 0.0 reduce-scatter.5.cloned.1.call-update
  214.1 0.0 reduce-scatter.3.cloned.1.call-start
  214.2 74.1 %all-gather.3.cloned.1.call-done = bf16[2,4096,1024]{2,1,0:T(8,128)(2,1)} async-done(((bf16[1,4096,1024]{2,1,0:T(8,128)(2,1)}), bf16[2,4096,1024]{2,1,0:T(8,128)(2,1)}) %all-gather.3.cloned.1.call-update) | async-done | bytes 16777232 | tf_op jit(solution)/shard_map/all_gather | solution.py:30
  288.3 29.6 %convolution_convert_fusion.1 = bf16[512,8192]{1,0:T(8,128)(2,1)} fusion(bf16[8192,1024]{1,0:T(8,128)(2,1)} %bitcast.26, bf16[1,512,1024]{2,1,0:T(8,128)(2,1)S(1)} %copy-done), kind=kOutput, calls=%fused_computation.1 | convolution fusion | flops 8594128896 | bytes 26214400 | tf_op jit(solution)/shard_map/dot_general | solution.py:34
  318.0 0.0 copy-start.3
  318.0 0.0 copy-start.4
  318.0 0.0 reduce-scatter.3.cloned.1.call-update
  318.0 0.0 all-gather.5.cloned.1.call-start
  318.0 147.7 %reduce-scatter.5.cloned.1.call-done = bf16[256,1024]{1,0:T(8,128)(2,1)} async-done(((bf16[8192,1024]{1,0:T(8,128)(2,1)}), bf16[256,1024]{1,0:T(8,128)(2,1)}) %reduce-scatter.5.cloned.1.call-update) | async-done | bytes 524304 | tf_op jit(solution)/shard_map/reduce_scatter | solution.py:49
  465.8 0.0 copy-done.3
  465.8 0.0 copy-done.4
  465.8 3.9 fusion.7
  469.7 0.0 all-gather.5.cloned.1.call-update
  469.7 93.4 %reduce-scatter.3.cloned.1.call-done = bf16[128,8192]{1,0:T(8,128)(2,1)} async-done(((bf16[512,8192]{1,0:T(8,128)(2,1)}), bf16[128,8192]{1,0:T(8,128)(2,1)}) %reduce-scatter.3.cloned.1.call-update) | async-done | bytes 2097168 | tf_op jit(solution)/shard_map/reduce_scatter | solution.py:33
  563.1 3.4 reshape.54
  566.5 2.8 collective-permute-start
  569.3 0.5 slice_bitcast_fusion
  569.8 3.2 collective-permute-done
  573.0 1.5 pad_maximum_fusion
  574.5 2.3 copy.12
  576.8 0.0 copy-done.1
  (3 shorter events, 0.0 us)
Async XLA Ops:
  8.0 190.2 %copy-start = (bf16[1,512,1024]{2,1,0:T(8,128)(2,1)S(1)}, bf16[1,512,1024]{2,1,0:T(8,128)(2,1)}, u32[]{:S(2)}) copy-start(bf16[1,512,1024]{2,1,0:T(8,128)(2,1)} %param.7) | copy-start | bytes 3145732
  8.0 1.7 copy-start.2
  8.0 280.3 %all-gather.3.cloned.1.call-start = ((), (), s32[]{:S(2)}) async-start(), calls=%async_computation.3 | async-start | bytes 25165824 | tf_op jit(solution)/shard_map/all_gather | solution.py:30
  8.8 457.0 %reduce-scatter.5.cloned.1.call-start = ((), (), s32[]{:S(2)}) async-start(), calls=%async_computation.5 | async-start | bytes 17301504 | tf_op jit(solution)/shard_map/reduce_scatter | solution.py:49
  214.1 348.9 %reduce-scatter.3.cloned.1.call-start = ((), (), s32[]{:S(2)}) async-start(), calls=%async_computation.4 | async-start | bytes 10485760 | tf_op jit(solution)/shard_map/reduce_scatter | solution.py:33
  318.0 147.8 %copy-start.3 = (f32[1,256,1024]{2,1,0:T(8,128)S(1)}, f32[1,256,1024]{2,1,0:T(8,128)}, u32[]{:S(2)}) copy-start(f32[1,256,1024]{2,1,0:T(8,128)} %param.9) | copy-start | bytes 3145732
  318.0 147.8 %copy-start.4 = (f32[1,256,1024]{2,1,0:T(8,128)S(1)}, f32[1,256,1024]{2,1,0:T(8,128)}, u32[]{:S(2)}) copy-start(f32[1,256,1024]{2,1,0:T(8,128)} %param.10) | copy-start | bytes 3145732
  318.0 256.5 %all-gather.5.cloned.1.call-start = ((), (), s32[]{:S(2)}) async-start(), calls=%async_computation.6 | async-start | bytes 1572864 | tf_op jit(solution)/shard_map/all_gather | solution.py:63
  465.8 111.0 %copy-start.1 = (bf16[1,512,1024]{2,1,0:T(8,128)(2,1)S(1)}, bf16[1,512,1024]{2,1,0:T(8,128)(2,1)}, u32[]{:S(2)}) copy-start(bf16[1,512,1024]{2,1,0:T(8,128)(2,1)} %param.7) | copy-start | bytes 3145732
  566.5 6.6 %collective-permute-start = (bf16[3,2048]{1,0:T(4,128)(2,1)S(1)}, bf16[3,2048]{1,0:T(4,128)(2,1)S(1)}, u32[]{:S(2)}, u32[]{:S(2)}) collective-permute-start(bf16[3,2048]{1,0:T(4,128)(2,1)S(1)} %slice.18), channel_id=1, source_target_pairs={{1,0},{2,1},{3,2},{4,3},{5,4},{6,5},{7,6},{8,7},{9,8},{10,9},{11,1... | collective-permute-start | bytes 36872 | tf_op jit(solution)/shard_map/ppermute | solution.py:20
Sparse Core Ops, SparseCore 0:
  10.5 277.7 all-gather.2
  469.8 40.4 all-gather.4
Sparse Core Ops, SparseCore 1:
  214.2 251.5 reduce-scatter.4
  468.3 94.7 reduce-scatter.2
